TPU v7x, 32 devices: a whole 2x2x4 slice. The times are simulated.
32 devices in a mesh: grp: 2 (over y), wide: 16 (over z, x, core).
Axes of the slice: x: 2, y: 2, z: 4, core: 2. Of those that a mesh axis runs over, the one named last changes fastest.
Arguments:
- tokens: bfloat16 [32, 768, 384], P(('grp', 'wide')), parts along dimension 0, may hold values from -6 to 6
- row_gain: float32 [384], replicated, may hold values from 0.25 to 1.75
- row_qkv: bfloat16 [384, 1152], replicated, may hold values from -10 to 10
- row_out: bfloat16 [384, 384], replicated, may hold values from -0.3125 to 0.3125
- col_gain: float32 [384], replicated, may hold values from 0.25 to 1.75
- col_qkv: bfloat16 [384, 1152], replicated, may hold values from -10 to 10
- col_out: bfloat16 [384, 384], replicated, may hold values from -0.3125 to 0.3125
Outputs:
- result: bfloat16 [32, 768, 384], P(('grp', 'wide')), parts along dimension 0
There are 2 independent parts, one for each index of `grp`. A program takes and returns all parts, laid end to end along the dimension named above; an argument that names none is the same for every part. Nothing has to cross between parts.
All inputs are finite; a program needn't handle non-finite values.
Results may differ from a plain program's by a relative error of at most 0.0075.
Values may be sent and summed in bfloat16 or wider, within the bound.
A program may use at most 64 MiB of HBM per device.

v0:
```python
import functools
import math

import jax
import jax.numpy as jnp
from jax import lax
from jax.experimental import pallas as pl
from jax.experimental.pallas import tpu as pltpu
from jax.sharding import PartitionSpec as P

HEADS = 6
AXIS = "wide"
TILE = 16
MESH = pl.DeviceIdType.MESH


def normalize(values, gain):
    floats = values.astype(jnp.float32)
    scale = lax.rsqrt(jnp.mean(floats * floats, axis=-1, keepdims=True) + 1e-06)
    return (floats * scale * gain).astype(jnp.bfloat16)


def attend(packed):
    channels = packed.shape[-1] // 3
    head_size = channels // HEADS
    shape = packed.shape[:2] + (HEADS, head_size)
    query = packed[..., :channels].reshape(shape)
    keys = packed[..., channels : 2 * channels].reshape(shape)
    values = packed[..., 2 * channels :].reshape(shape)
    scores = jnp.einsum(
        "qbhd,kbhd->bhqk", query, keys, preferred_element_type=jnp.float32
    ) * head_size ** (-0.5)
    scores = scores - jnp.max(scores, axis=-1, keepdims=True)
    expo = jnp.exp(scores)
    weights = (expo / jnp.sum(expo, axis=-1, keepdims=True)).astype(jnp.bfloat16)
    mixed = jnp.einsum("bhqk,kbhd->qbhd", weights, values, preferred_element_type=jnp.float32)
    return mixed.reshape(packed.shape[:2] + (channels,)).astype(jnp.bfloat16)


def project(flat, weight):
    return jnp.dot(flat, weight, preferred_element_type=jnp.float32).astype(jnp.bfloat16)


def residual_add(base, mixed, weight):
    rows, columns, channels = base.shape
    update = jnp.dot(
        mixed.reshape(rows * columns, channels), weight, preferred_element_type=jnp.float32
    )
    return (base.astype(jnp.float32) + update.reshape(base.shape)).astype(jnp.bfloat16)


def plain(tokens, row_gain, row_qkv, row_out, col_gain, col_qkv, col_out):
    rows, columns, channels = tokens.shape
    normed = normalize(tokens, row_gain).reshape(rows * columns, channels)
    packed = project(normed, row_qkv).reshape(rows, columns, 3 * channels)
    mixed = lax.map(lambda one_row: attend(one_row[:, None, :])[:, 0, :], packed)
    first = residual_add(tokens, mixed, row_out)
    moved = lax.all_to_all(first, AXIS, split_axis=1, concat_axis=0, tiled=True)
    length, count, _ = moved.shape
    flat = normalize(moved, col_gain).reshape(length * count, channels)
    column_mixed = attend(project(flat, col_qkv).reshape(length, count, 3 * channels))
    returned = lax.all_to_all(column_mixed, AXIS, split_axis=0, concat_axis=1, tiled=True)
    return residual_add(first, returned, col_out)


def kernel(
    x_hbm, rg_hbm, rqkv_hbm, rout_hbm, cg_hbm, cqkv_hbm, cout_hbm,
    out_ref,
    rg_ref, cg_ref, x_ref, rkv_ref, rq_ref, rout_ref, cqkv_ref, cout_ref,
    n_ref, k_ref, v_ref, cv_ref, send_ref, recv_ref, back_ref,
    load_sem, own_sem, s1_sem, r1_sem, s2_sem, r2_sem,
):
    n, _, channels = x_hbm.shape
    chunks = x_ref.shape[0]
    size = n * TILE
    half = n // 2
    head = channels // HEADS
    per = 128 // head
    pairs = channels // 128
    me = lax.axis_index(AXIS)
    mine = me // half
    other = 1 - mine

    loads = [
        pltpu.make_async_copy(
            x_hbm.at[:, pl.ds(c * TILE, TILE), :], x_ref.at[c], load_sem.at[c]
        )
        for c in range(chunks)
    ]
    weights = [
        pltpu.make_async_copy(src, dst, load_sem.at[chunks + i])
        for i, (src, dst) in enumerate(
            [
                (rg_hbm, rg_ref.at[0]),
                (rqkv_hbm.at[:, pl.ds(channels, 2 * channels)], rkv_ref),
                (rqkv_hbm.at[:, pl.ds(0, channels)], rq_ref),
                (rout_hbm, rout_ref),
                (cg_hbm, cg_ref.at[0]),
                (cqkv_hbm, cqkv_ref),
                (cout_hbm, cout_ref),
            ]
        )
    ]
    for copy in [loads[0]] + weights[:2] + loads[1:] + weights[2:4]:
        copy.start()

    barrier = pltpu.get_barrier_semaphore()

    def greet(j, carry):
        peer = lax.rem(me + j, n)
        pl.semaphore_signal(barrier, inc=1, device_id={AXIS: peer}, device_id_type=MESH)
        return carry

    lax.fori_loop(1, n, greet, 0)

    factor = head ** (-0.5) * math.log2(math.e)
    ones = jnp.ones((size, 128), jnp.bfloat16)

    def attention(query, keys, values, mask):
        mixed = None
        lane = lax.broadcasted_iota(jnp.int32, query.shape, 1)
        for h in range(per):
            part = (lane >= h * head) & (lane < (h + 1) * head)
            one = jnp.where(part, query, jnp.zeros_like(query))
            scores = lax.dot_general(
                one, keys, (((1,), (1,)), ((), ())), preferred_element_type=jnp.float32
            )
            if mask is not None:
                scores = jnp.where(mask, scores, -jnp.inf)
            peak = jnp.max(scores, axis=-1, keepdims=True)
            expo = jnp.exp2(scores - peak).astype(jnp.bfloat16)
            both = jnp.dot(expo, values, preferred_element_type=jnp.float32)
            own = both[:, :128] / both[:, 128:]
            mixed = own if mixed is None else jnp.where(part, own, mixed)
        return mixed.astype(jnp.bfloat16)

    for c in range(chunks):
        loads[c].wait()
        if c == 0:
            weights[0].wait()
            weights[1].wait()
        normed = normalize(x_ref[c].reshape(size, channels), rg_ref[...])
        n_ref[c] = normed.reshape(n, TILE, channels)
        packed = jnp.dot(normed, rkv_ref[...], preferred_element_type=jnp.float32)
        k_ref[pl.ds(c * size, size), :] = packed[:, :channels].astype(jnp.bfloat16)
        for p in range(pairs):
            at = channels + p * 128
            v_ref[p, pl.ds(c * size, size), :128] = packed[:, at : at + 128].astype(jnp.bfloat16)
            v_ref[p, pl.ds(c * size, size), 128:] = ones
    for p in range(pairs):
        cv_ref[p, :, 128:] = ones
    for copy in weights[4:]:
        copy.start()
    weights[2].wait()
    weights[3].wait()

    def copy_out(c, peer):
        return pltpu.make_async_remote_copy(
            src_ref=send_ref.at[c, peer], dst_ref=recv_ref.at[c, me],
            send_sem=s1_sem.at[c, peer], recv_sem=r1_sem.at[c, me],
            device_id={AXIS: peer}, device_id_type=MESH,
        )

    def copy_in(c, peer):
        return pltpu.make_async_remote_copy(
            src_ref=send_ref.at[c, peer], dst_ref=recv_ref.at[c, peer],
            send_sem=s1_sem.at[c, peer], recv_sem=r1_sem.at[c, peer],
            device_id={AXIS: peer}, device_id_type=MESH,
        )

    def back_out(c, peer):
        return pltpu.make_async_remote_copy(
            src_ref=back_ref.at[c, peer], dst_ref=out_ref.at[me, pl.ds(c * TILE, TILE), :],
            send_sem=s2_sem.at[c, peer], recv_sem=r2_sem.at[c, me],
            device_id={AXIS: peer}, device_id_type=MESH,
        )

    def back_in(c, peer):
        return pltpu.make_async_remote_copy(
            src_ref=back_ref.at[c, peer], dst_ref=out_ref.at[peer, pl.ds(c * TILE, TILE), :],
            send_sem=s2_sem.at[c, peer], recv_sem=r2_sem.at[c, peer],
            device_id={AXIS: peer}, device_id_type=MESH,
        )

    def across(body, lo=0, hi=half):
        def step(j, carry):
            body(other * half + j)
            return carry

        lax.fori_loop(lo, hi, step, 0)

    def along(body):
        def step(j, carry):
            body(mine * half + lax.rem(me + j, half))
            return carry

        lax.fori_loop(1, half, step, 0)

    def peers(body):
        across(body)
        along(body)

    def row_unit(c, start, count):
        at = pl.ds(start, count)
        normed = n_ref[c, at].reshape(count * TILE, channels)
        query = jnp.dot(normed, rq_ref[...], preferred_element_type=jnp.float32)
        query = (query * factor).astype(jnp.bfloat16)
        mixed = jnp.concatenate(
            [
                attention(
                    query[:, p * 128 : (p + 1) * 128],
                    k_ref[:, p * 128 : (p + 1) * 128],
                    v_ref[p],
                    None,
                )
                for p in range(pairs)
            ],
            axis=1,
        )
        update = jnp.dot(mixed, rout_ref[...], preferred_element_type=jnp.float32)
        base = x_ref[c, at].reshape(count * TILE, channels).astype(jnp.float32)
        first = (base + update).astype(jnp.bfloat16)
        send_ref[c, at] = first.reshape(count, TILE, channels)

    def row_across(c, splits=1):
        count = half // splits
        for i in range(splits):
            row_unit(c, other * half + i * count, count)
            if i == 0 and splits > 1:
                pl.semaphore_wait(barrier, n - 1)
            across(lambda peer: copy_out(c, peer).start(), i * count, (i + 1) * count)

    def row_along(c):
        row_unit(c, mine * half, half)
        along(lambda peer: copy_out(c, peer).start())
        recv_ref[c, me] = send_ref[c, me]

    def row_step(c, carry):
        row_across(c)
        row_along(c - 1)
        return carry

    row_across(0, 2)
    lax.fori_loop(1, chunks, row_step, 0)
    row_along(chunks - 1)
    for copy in weights[4:]:
        copy.wait()

    at_row = lax.broadcasted_iota(jnp.int32, (size, size), 0)
    at_col = lax.broadcasted_iota(jnp.int32, (size, size), 1)
    same = lax.rem(at_row, TILE) == lax.rem(at_col, TILE)

    def col_chunk(c, carry):
        peers(lambda peer: copy_in(c, peer).wait_recv())
        base = recv_ref[c].reshape(size, channels)
        normed = normalize(base, cg_ref[...])
        packed = jnp.dot(normed, cqkv_ref[...], preferred_element_type=jnp.float32)
        query = (packed[:, :channels] * factor).astype(jnp.bfloat16)
        keys = packed[:, channels : 2 * channels].astype(jnp.bfloat16)
        for p in range(pairs):
            at = 2 * channels + p * 128
            cv_ref[p, :, :128] = packed[:, at : at + 128].astype(jnp.bfloat16)
        mixed = jnp.concatenate(
            [
                attention(
                    query[:, p * 128 : (p + 1) * 128],
                    keys[:, p * 128 : (p + 1) * 128],
                    cv_ref[p],
                    same,
                )
                for p in range(pairs)
            ],
            axis=1,
        )
        update = jnp.dot(mixed, cout_ref[...], preferred_element_type=jnp.float32)
        result = (base.astype(jnp.float32) + update).astype(jnp.bfloat16)
        back_ref[c] = result.reshape(n, TILE, channels)
        peers(lambda peer: back_out(c, peer).start())
        pltpu.make_async_copy(
            back_ref.at[c, me], out_ref.at[me, pl.ds(c * TILE, TILE), :], own_sem.at[c]
        ).start()
        return carry

    lax.fori_loop(0, chunks, col_chunk, 0)

    def finish(c, carry):
        pltpu.make_async_copy(
            back_ref.at[c, me], out_ref.at[me, pl.ds(c * TILE, TILE), :], own_sem.at[c]
        ).wait()
        peers(lambda peer: copy_out(c, peer).wait_send())
        peers(lambda peer: back_out(c, peer).wait_send())
        peers(lambda peer: back_in(c, peer).wait_recv())
        return carry

    lax.fori_loop(0, chunks, finish, 0)


def fused(n, tokens, row_gain, row_qkv, row_out, col_gain, col_qkv, col_out):
    _, columns, channels = tokens.shape
    chunks = columns // (n * TILE)
    size = n * TILE
    pairs = channels // 128
    bf16 = jnp.bfloat16
    hbm = pl.BlockSpec(memory_space=pl.ANY)
    dma = pltpu.SemaphoreType.DMA
    flops = 2 * columns * channels * (8 * channels + 2 * columns + 2 * size)
    out = pl.pallas_call(
        kernel,
        out_shape=pltpu.VMEM((n, columns // n, channels), bf16),
        in_specs=[hbm] * 7,
        out_specs=pl.BlockSpec(memory_space=pltpu.VMEM),
        scratch_shapes=[
            pltpu.VMEM((1, channels), jnp.float32),
            pltpu.VMEM((1, channels), jnp.float32),
            pltpu.VMEM((chunks, n, TILE, channels), bf16),
            pltpu.VMEM((channels, 2 * channels), bf16),
            pltpu.VMEM((channels, channels), bf16),
            pltpu.VMEM((channels, channels), bf16),
            pltpu.VMEM((channels, 3 * channels), bf16),
            pltpu.VMEM((channels, channels), bf16),
            pltpu.VMEM((chunks, n, TILE, channels), bf16),
            pltpu.VMEM((columns, channels), bf16),
            pltpu.VMEM((pairs, columns, 256), bf16),
            pltpu.VMEM((pairs, size, 256), bf16),
            pltpu.VMEM((chunks, n, TILE, channels), bf16),
            pltpu.VMEM((chunks, n, TILE, channels), bf16),
            pltpu.VMEM((chunks, n, TILE, channels), bf16),
            dma((chunks + 7,)),
            dma((chunks,)),
            dma((chunks, n)),
            dma((chunks, n)),
            dma((chunks, n)),
            dma((chunks, n)),
        ],
        compiler_params=pltpu.CompilerParams(
            collective_id=0, has_side_effects=True, vmem_limit_bytes=60000000
        ),
        cost_estimate=pl.CostEstimate(
            flops=flops, bytes_accessed=8 * columns * channels, transcendentals=0
        ),
    )(
        tokens.reshape(n, columns // n, channels),
        row_gain,
        row_qkv,
        row_out,
        col_gain,
        col_qkv,
        col_out,
    )
    return out.reshape(tokens.shape)


def solution(mesh):
    n = mesh.shape[AXIS]

    def body(tokens, *rest):
        rows, columns, channels = tokens.shape
        whole_tiles = rows == 1 and columns % (n * TILE) == 0 and channels % 128 == 0
        if n % 4 == 0 and whole_tiles and 128 % (channels // HEADS) == 0:
            return fused(n, tokens, *rest)
        return plain(tokens, *rest)

    in_specs = (P(("grp", AXIS), None, None), P(), P(), P(), P(), P(), P())
    out_specs = P(("grp", AXIS), None, None)
    return jax.shard_map(body, mesh=mesh, in_specs=in_specs, out_specs=out_specs, check_vma=False)
```

profile of v0, /device:TPU:0, one launch (start us, length us, event | category | flops | bytes accessed | tf_op | source)
XLA Modules:
  0.0 36.6 jit_solution(6617929309085871501)
XLA Ops:
  0.0 35.8 %shard_map.73 = bf16[16,48,384]{2,1,0:T(8,128)(2,1)S(1)} custom-call(bf16[16,48,384]{2,1,0:T(8,128)(2,1)} %bitcast.3, f32[384]{0:T(512)} %rg_hbm.1, bf16[384,1152]{1,0:T(8,128)(2,1)} %rqkv_hbm.1, bf16[384,384]{1,0:T(8,128)(2,1)} %rout_hbm.1, f32[384]{0:T(512)} %cg_hbm.1, bf16[384,1152]{1,0:T(8,128)(2,1)} %cqkv_hbm.1, bf16[384,384]{1,0:T(8,128)(2,1)} %cout_hbm.1), custom_call_target="tpu_custom_call" | custom-call | flops 3019898880 | bytes 2359296 | tf_op jit(solution)/shard_map/pallas_call | solution.py:307
  35.8 0.8 %copy.9 = bf16[1,768,384]{2,1,0:T(8,128)(2,1)} copy(bf16[1,768,384]{2,1,0:T(8,128)(2,1)S(1)} %bitcast.2) | data formatting | bytes 1179648
where the time goes:
time: 36.8 us; the launch traced here: 36.6 us
  Pallas kernels  35.8 us (97%)
  local copies, waits for them, and re-layouts  0.82 us (2%)
    pallas_call x1, Pallas kernels, fused(): pl.pallas_call(kernel, out_shape=pltpu.VMEM((n, columns // n, channels),...  35.8 us
    unnamed x1, local copies, waits for them, and re-layouts  0.82 us

commit v1 on v0

--- a/solution.py
+++ b/solution.py
@@ -68,7 +68,7 @@
     out_ref,
     rg_ref, cg_ref, x_ref, rkv_ref, rq_ref, rout_ref, cqkv_ref, cout_ref,
     n_ref, k_ref, v_ref, cv_ref, send_ref, recv_ref, back_ref,
-    load_sem, own_sem, s1_sem, r1_sem, s2_sem, r2_sem,
+    load_sem, sent_sem, r1_sem, r2_sem,
 ):
     n, _, channels = x_hbm.shape
     chunks = x_ref.shape[0]
@@ -134,11 +134,9 @@
             mixed = own if mixed is None else jnp.where(part, own, mixed)
         return mixed.astype(jnp.bfloat16)
 
+    for copy in loads + weights[:2]:
+        copy.wait()
     for c in range(chunks):
-        loads[c].wait()
-        if c == 0:
-            weights[0].wait()
-            weights[1].wait()
         normed = normalize(x_ref[c].reshape(size, channels), rg_ref[...])
         n_ref[c] = normed.reshape(n, TILE, channels)
         packed = jnp.dot(normed, rkv_ref[...], preferred_element_type=jnp.float32)
@@ -157,28 +155,18 @@
     def copy_out(c, peer):
         return pltpu.make_async_remote_copy(
             src_ref=send_ref.at[c, peer], dst_ref=recv_ref.at[c, me],
-            send_sem=s1_sem.at[c, peer], recv_sem=r1_sem.at[c, me],
+            send_sem=sent_sem, recv_sem=r1_sem.at[c],
             device_id={AXIS: peer}, device_id_type=MESH,
         )
 
-    def copy_in(c, peer):
-        return pltpu.make_async_remote_copy(
-            src_ref=send_ref.at[c, peer], dst_ref=recv_ref.at[c, peer],
-            send_sem=s1_sem.at[c, peer], recv_sem=r1_sem.at[c, peer],
-            device_id={AXIS: peer}, device_id_type=MESH,
-        )
+    def copies_in(c):
+        whole = recv_ref.at[c, pl.ds(0, n - 1)]
+        return pltpu.make_async_copy(whole, whole, r1_sem.at[c])
 
     def back_out(c, peer):
         return pltpu.make_async_remote_copy(
             src_ref=back_ref.at[c, peer], dst_ref=out_ref.at[me, pl.ds(c * TILE, TILE), :],
-            send_sem=s2_sem.at[c, peer], recv_sem=r2_sem.at[c, me],
-            device_id={AXIS: peer}, device_id_type=MESH,
-        )
-
-    def back_in(c, peer):
-        return pltpu.make_async_remote_copy(
-            src_ref=back_ref.at[c, peer], dst_ref=out_ref.at[peer, pl.ds(c * TILE, TILE), :],
-            send_sem=s2_sem.at[c, peer], recv_sem=r2_sem.at[c, peer],
+            send_sem=sent_sem, recv_sem=r2_sem,
             device_id={AXIS: peer}, device_id_type=MESH,
         )
 
@@ -251,7 +239,7 @@
     same = lax.rem(at_row, TILE) == lax.rem(at_col, TILE)
 
     def col_chunk(c, carry):
-        peers(lambda peer: copy_in(c, peer).wait_recv())
+        copies_in(c).wait()
         base = recv_ref[c].reshape(size, channels)
         normed = normalize(base, cg_ref[...])
         packed = jnp.dot(normed, cqkv_ref[...], preferred_element_type=jnp.float32)
@@ -276,23 +264,17 @@
         result = (base.astype(jnp.float32) + update).astype(jnp.bfloat16)
         back_ref[c] = result.reshape(n, TILE, channels)
         peers(lambda peer: back_out(c, peer).start())
-        pltpu.make_async_copy(
-            back_ref.at[c, me], out_ref.at[me, pl.ds(c * TILE, TILE), :], own_sem.at[c]
-        ).start()
+        out_ref[me, pl.ds(c * TILE, TILE), :] = back_ref[c, me]
         return carry
 
     lax.fori_loop(0, chunks, col_chunk, 0)
 
-    def finish(c, carry):
-        pltpu.make_async_copy(
-            back_ref.at[c, me], out_ref.at[me, pl.ds(c * TILE, TILE), :], own_sem.at[c]
-        ).wait()
-        peers(lambda peer: copy_out(c, peer).wait_send())
-        peers(lambda peer: back_out(c, peer).wait_send())
-        peers(lambda peer: back_in(c, peer).wait_recv())
-        return carry
-
-    lax.fori_loop(0, chunks, finish, 0)
+    out_part = out_ref.at[pl.ds(0, n - 1)]
+    send_part = send_ref.at[:, pl.ds(0, n - 1)]
+    back_part = back_ref.at[:, pl.ds(0, n - 1)]
+    pltpu.make_async_copy(send_part, send_part, sent_sem).wait()
+    pltpu.make_async_copy(back_part, back_part, sent_sem).wait()
+    pltpu.make_async_copy(out_part, out_part, r2_sem).wait()
 
 
 def fused(n, tokens, row_gain, row_qkv, row_out, col_gain, col_qkv, col_out):
@@ -326,11 +308,9 @@
             pltpu.VMEM((chunks, n, TILE, channels), bf16),
             pltpu.VMEM((chunks, n, TILE, channels), bf16),
             dma((chunks + 7,)),
+            dma(()),
             dma((chunks,)),
-            dma((chunks, n)),
-            dma((chunks, n)),
-            dma((chunks, n)),
-            dma((chunks, n)),
+            dma(()),
         ],
         compiler_params=pltpu.CompilerParams(
             collective_id=0, has_side_effects=True, vmem_limit_bytes=60000000

time: 36.8 us -> 34.5 us (0.938)
  Pallas kernels: 35.8 us -> 33.6 us
    pallas_call x1, Pallas kernels: 35.8 us -> 33.6 us  [fused(): pl.pallas_call(kernel, out_shape=pltpu.VMEM((n, columns // n, channels),...]
where the time goes in v1:
time: 34.5 us; the launch traced here: 34.4 us
  Pallas kernels  33.6 us (97%)
  local copies, waits for them, and re-layouts  0.82 us (2%)
    pallas_call x1, Pallas kernels, fused(): pl.pallas_call(kernel, out_shape=pltpu.VMEM((n, columns // n, channels),...  33.6 us
    unnamed x1, local copies, waits for them, and re-layouts  0.82 us

profile of v1, /device:TPU:0, one launch (start us, length us, event | category | flops | bytes accessed | tf_op | source)
XLA Modules:
  0.0 34.4 jit_solution(4226524870688130930)
XLA Ops:
  0.0 33.6 %shard_map.73 = bf16[16,48,384]{2,1,0:T(8,128)(2,1)S(1)} custom-call(bf16[16,48,384]{2,1,0:T(8,128)(2,1)} %bitcast.3, f32[384]{0:T(512)} %rg_hbm.1, bf16[384,1152]{1,0:T(8,128)(2,1)} %rqkv_hbm.1, bf16[384,384]{1,0:T(8,128)(2,1)} %rout_hbm.1, f32[384]{0:T(512)} %cg_hbm.1, bf16[384,1152]{1,0:T(8,128)(2,1)} %cqkv_hbm.1, bf16[384,384]{1,0:T(8,128)(2,1)} %cout_hbm.1), custom_call_target="tpu_custom_call" | custom-call | flops 3019898880 | bytes 2359296 | tf_op jit(solution)/shard_map/pallas_call | solution.py:289
  33.6 0.8 %copy.9 = bf16[1,768,384]{2,1,0:T(8,128)(2,1)} copy(bf16[1,768,384]{2,1,0:T(8,128)(2,1)S(1)} %bitcast.2) | data formatting | bytes 1179648

commit v2 on v1

--- a/solution.py
+++ b/solution.py
@@ -74,6 +74,7 @@
     chunks = x_ref.shape[0]
     size = n * TILE
     half = n // 2
+    early = 2
     head = channels // HEADS
     per = 128 // head
     pairs = channels // 128
@@ -101,7 +102,7 @@
             ]
         )
     ]
-    for copy in [loads[0]] + weights[:2] + loads[1:] + weights[2:4]:
+    for copy in weights[:1] + loads + weights[1:4]:
         copy.start()
 
     barrier = pltpu.get_barrier_semaphore()
@@ -117,28 +118,33 @@
     ones = jnp.ones((size, 128), jnp.bfloat16)
 
     def attention(query, keys, values, mask):
-        mixed = None
-        lane = lax.broadcasted_iota(jnp.int32, query.shape, 1)
-        for h in range(per):
-            part = (lane >= h * head) & (lane < (h + 1) * head)
-            one = jnp.where(part, query, jnp.zeros_like(query))
-            scores = lax.dot_general(
-                one, keys, (((1,), (1,)), ((), ())), preferred_element_type=jnp.float32
-            )
-            if mask is not None:
-                scores = jnp.where(mask, scores, -jnp.inf)
-            peak = jnp.max(scores, axis=-1, keepdims=True)
-            expo = jnp.exp2(scores - peak).astype(jnp.bfloat16)
-            both = jnp.dot(expo, values, preferred_element_type=jnp.float32)
-            own = both[:, :128] / both[:, 128:]
-            mixed = own if mixed is None else jnp.where(part, own, mixed)
+        count = query.shape[0]
+        lane = lax.broadcasted_iota(jnp.int32, query.shape, 1) // head
+        apart = jnp.concatenate(
+            [jnp.where(lane == h, query, jnp.zeros_like(query)) for h in range(per)], axis=0
+        )
+        scores = lax.dot_general(
+            apart, keys, (((1,), (1,)), ((), ())), preferred_element_type=jnp.float32
+        )
+        if mask is not None:
+            scores = jnp.where(mask, scores, -jnp.inf)
+        peak = jnp.max(scores, axis=-1, keepdims=True)
+        expo = jnp.exp2(scores - peak).astype(jnp.bfloat16)
+        both = jnp.dot(expo, values, preferred_element_type=jnp.float32)
+        both = both[:, :128] / both[:, 128:]
+        mixed = both[:count]
+        for h in range(1, per):
+            mixed = jnp.where(lane == h, both[h * count : (h + 1) * count], mixed)
         return mixed.astype(jnp.bfloat16)
 
-    for copy in loads + weights[:2]:
+    for copy in loads + weights[:1]:
         copy.wait()
     for c in range(chunks):
         normed = normalize(x_ref[c].reshape(size, channels), rg_ref[...])
         n_ref[c] = normed.reshape(n, TILE, channels)
+    weights[1].wait()
+    for c in range(chunks):
+        normed = n_ref[c].reshape(size, channels)
         packed = jnp.dot(normed, rkv_ref[...], preferred_element_type=jnp.float32)
         k_ref[pl.ds(c * size, size), :] = packed[:, :channels].astype(jnp.bfloat16)
         for p in range(pairs):
@@ -184,9 +190,18 @@
 
         lax.fori_loop(1, half, step, 0)
 
-    def peers(body):
-        across(body)
-        along(body)
+    def send_back(c, lo, hi):
+        def skip(j):
+            return mine * half + j + jnp.where(j >= me - mine * half, 1, 0)
+
+        def step(k, carry):
+            lower = jnp.where(k < half, k, skip(k - half))
+            upper = jnp.where(k < half + early, half + lax.rem((k - early) * (half // 2) + (k - early) // 2, half), skip(k - half))
+            upper = jnp.where(k < early, skip(k), upper)
+            back_out(c, jnp.where(mine == 1, lower, upper)).start()
+            return carry
+
+        lax.fori_loop(lo, hi, step, 0)
 
     def row_unit(c, start, count):
         at = pl.ds(start, count)
@@ -234,8 +249,8 @@
     for copy in weights[4:]:
         copy.wait()
 
-    at_row = lax.broadcasted_iota(jnp.int32, (size, size), 0)
-    at_col = lax.broadcasted_iota(jnp.int32, (size, size), 1)
+    at_row = lax.broadcasted_iota(jnp.int32, (per * size, size), 0)
+    at_col = lax.broadcasted_iota(jnp.int32, (per * size, size), 1)
     same = lax.rem(at_row, TILE) == lax.rem(at_col, TILE)
 
     def col_chunk(c, carry):
@@ -263,11 +278,18 @@
         update = jnp.dot(mixed, cout_ref[...], preferred_element_type=jnp.float32)
         result = (base.astype(jnp.float32) + update).astype(jnp.bfloat16)
         back_ref[c] = result.reshape(n, TILE, channels)
-        peers(lambda peer: back_out(c, peer).start())
+
+        @pl.when(c < chunks - 2)
+        def _():
+            send_back(c, 0, n - 1)
+
         out_ref[me, pl.ds(c * TILE, TILE), :] = back_ref[c, me]
         return carry
 
     lax.fori_loop(0, chunks, col_chunk, 0)
+    for lo, hi in [(0, early), (early, n - 1)]:
+        for c in range(max(chunks - 2, 0), chunks):
+            send_back(c, lo, hi)
 
     out_part = out_ref.at[pl.ds(0, n - 1)]
     send_part = send_ref.at[:, pl.ds(0, n - 1)]

time: 34.5 us -> 32.8 us (0.951)
  the two profiles are of different devices: /device:TPU:0 before, /device:TPU:9 now
where the time goes in v2:
time: 32.8 us; the launch traced here: 32.7 us
  Pallas kernels  31.9 us (97%)
  local copies, waits for them, and re-layouts  0.82 us (2%)
    pallas_call x1, Pallas kernels, fused(): pl.pallas_call(kernel, out_shape=pltpu.VMEM((n, columns // n, channels),...  31.9 us
    unnamed x1, local copies, waits for them, and re-layouts  0.82 us

profile of v2, /device:TPU:9, one launch (start us, length us, event | category | flops | bytes accessed | tf_op | source)
XLA Modules:
  0.0 32.7 jit_solution(8871754253616429917)
XLA Ops:
  0.0 31.9 %shard_map.73 = bf16[16,48,384]{2,1,0:T(8,128)(2,1)S(1)} custom-call(bf16[16,48,384]{2,1,0:T(8,128)(2,1)} %bitcast.3, f32[384]{0:T(512)} %rg_hbm.1, bf16[384,1152]{1,0:T(8,128)(2,1)} %rqkv_hbm.1, bf16[384,384]{1,0:T(8,128)(2,1)} %rout_hbm.1, f32[384]{0:T(512)} %cg_hbm.1, bf16[384,1152]{1,0:T(8,128)(2,1)} %cqkv_hbm.1, bf16[384,384]{1,0:T(8,128)(2,1)} %cout_hbm.1), custom_call_target="tpu_custom_call" | custom-call | flops 3019898880 | bytes 2359296 | tf_op jit(solution)/shard_map/pallas_call | solution.py:311
  31.9 0.8 %copy.9 = bf16[1,768,384]{2,1,0:T(8,128)(2,1)} copy(bf16[1,768,384]{2,1,0:T(8,128)(2,1)S(1)} %bitcast.2) | data formatting | bytes 1179648

commit v3 on v2

--- a/solution.py
+++ b/solution.py
@@ -66,7 +66,7 @@
 def kernel(
     x_hbm, rg_hbm, rqkv_hbm, rout_hbm, cg_hbm, cqkv_hbm, cout_hbm,
     out_ref,
-    rg_ref, cg_ref, x_ref, rkv_ref, rq_ref, rout_ref, cqkv_ref, cout_ref,
+    rg_ref, cg_ref, x_ref, rqkv_ref, rout_ref, cqkv_ref, cout_ref,
     n_ref, k_ref, v_ref, cv_ref, send_ref, recv_ref, back_ref,
     load_sem, sent_sem, r1_sem, r2_sem,
 ):
@@ -74,7 +74,8 @@
     chunks = x_ref.shape[0]
     size = n * TILE
     half = n // 2
-    early = 2
+    early = min(2, half - 1)
+    held = early + half // 4
     head = channels // HEADS
     per = 128 // head
     pairs = channels // 128
@@ -93,8 +94,7 @@
         for i, (src, dst) in enumerate(
             [
                 (rg_hbm, rg_ref.at[0]),
-                (rqkv_hbm.at[:, pl.ds(channels, 2 * channels)], rkv_ref),
-                (rqkv_hbm.at[:, pl.ds(0, channels)], rq_ref),
+                (rqkv_hbm, rqkv_ref),
                 (rout_hbm, rout_ref),
                 (cg_hbm, cg_ref.at[0]),
                 (cqkv_hbm, cqkv_ref),
@@ -102,7 +102,7 @@
             ]
         )
     ]
-    for copy in weights[:1] + loads + weights[1:4]:
+    for copy in weights[:1] + loads + weights[1:3]:
         copy.start()
 
     barrier = pltpu.get_barrier_semaphore()
@@ -114,8 +114,8 @@
 
     lax.fori_loop(1, n, greet, 0)
 
+    columns = k_ref.shape[0]
     factor = head ** (-0.5) * math.log2(math.e)
-    ones = jnp.ones((size, 128), jnp.bfloat16)
 
     def attention(query, keys, values, mask):
         count = query.shape[0]
@@ -137,26 +137,25 @@
             mixed = jnp.where(lane == h, both[h * count : (h + 1) * count], mixed)
         return mixed.astype(jnp.bfloat16)
 
-    for copy in loads + weights[:1]:
+    for p in range(pairs):
+        v_ref[p, :, 128:] = jnp.ones((columns, 128), jnp.bfloat16)
+        cv_ref[p, :, 128:] = jnp.ones((size, 128), jnp.bfloat16)
+    weights[0].wait()
+    for c in range(chunks):
+        loads[c].wait()
+        normed = normalize(x_ref[c].reshape(size, channels), rg_ref[...])
+        n_ref[c] = normed.reshape(n, TILE, channels)
+    for copy in weights[3:]:
+        copy.start()
+    for copy in weights[1:3]:
         copy.wait()
     for c in range(chunks):
-        normed = normalize(x_ref[c].reshape(size, channels), rg_ref[...])
-        n_ref[c] = normed.reshape(n, TILE, channels)
-    weights[1].wait()
-    for c in range(chunks):
         normed = n_ref[c].reshape(size, channels)
-        packed = jnp.dot(normed, rkv_ref[...], preferred_element_type=jnp.float32)
+        packed = jnp.dot(normed, rqkv_ref[:, channels:], preferred_element_type=jnp.float32)
         k_ref[pl.ds(c * size, size), :] = packed[:, :channels].astype(jnp.bfloat16)
         for p in range(pairs):
             at = channels + p * 128
             v_ref[p, pl.ds(c * size, size), :128] = packed[:, at : at + 128].astype(jnp.bfloat16)
-            v_ref[p, pl.ds(c * size, size), 128:] = ones
-    for p in range(pairs):
-        cv_ref[p, :, 128:] = ones
-    for copy in weights[4:]:
-        copy.start()
-    weights[2].wait()
-    weights[3].wait()
 
     def copy_out(c, peer):
         return pltpu.make_async_remote_copy(
@@ -206,7 +205,7 @@
     def row_unit(c, start, count):
         at = pl.ds(start, count)
         normed = n_ref[c, at].reshape(count * TILE, channels)
-        query = jnp.dot(normed, rq_ref[...], preferred_element_type=jnp.float32)
+        query = jnp.dot(normed, rqkv_ref[:, :channels], preferred_element_type=jnp.float32)
         query = (query * factor).astype(jnp.bfloat16)
         mixed = jnp.concatenate(
             [
@@ -246,7 +245,7 @@
     row_across(0, 2)
     lax.fori_loop(1, chunks, row_step, 0)
     row_along(chunks - 1)
-    for copy in weights[4:]:
+    for copy in weights[3:]:
         copy.wait()
 
     at_row = lax.broadcasted_iota(jnp.int32, (per * size, size), 0)
@@ -279,17 +278,16 @@
         result = (base.astype(jnp.float32) + update).astype(jnp.bfloat16)
         back_ref[c] = result.reshape(n, TILE, channels)
 
-        @pl.when(c < chunks - 2)
-        def _():
-            send_back(c, 0, n - 1)
+        ready = jnp.where((c < chunks - 2) | (mine == 0), n - 1, held)
+        send_back(c, 0, jnp.where(c == chunks - 1, early, ready))
 
         out_ref[me, pl.ds(c * TILE, TILE), :] = back_ref[c, me]
         return carry
 
     lax.fori_loop(0, chunks, col_chunk, 0)
-    for lo, hi in [(0, early), (early, n - 1)]:
-        for c in range(max(chunks - 2, 0), chunks):
-            send_back(c, lo, hi)
+    if chunks > 1:
+        send_back(chunks - 2, jnp.where(mine == 0, n - 1, held), n - 1)
+    send_back(chunks - 1, early, n - 1)
 
     out_part = out_ref.at[pl.ds(0, n - 1)]
     send_part = send_ref.at[:, pl.ds(0, n - 1)]
@@ -317,8 +315,7 @@
             pltpu.VMEM((1, channels), jnp.float32),
             pltpu.VMEM((1, channels), jnp.float32),
             pltpu.VMEM((chunks, n, TILE, channels), bf16),
-            pltpu.VMEM((channels, 2 * channels), bf16),
-            pltpu.VMEM((channels, channels), bf16),
+            pltpu.VMEM((channels, 3 * channels), bf16),
             pltpu.VMEM((channels, channels), bf16),
             pltpu.VMEM((channels, 3 * channels), bf16),
             pltpu.VMEM((channels, channels), bf16),
@@ -329,7 +326,7 @@
             pltpu.VMEM((chunks, n, TILE, channels), bf16),
             pltpu.VMEM((chunks, n, TILE, channels), bf16),
             pltpu.VMEM((chunks, n, TILE, channels), bf16),
-            dma((chunks + 7,)),
+            dma((chunks + 6,)),
             dma(()),
             dma((chunks,)),
             dma(()),

time: 32.8 us -> 32.7 us (level)
  no operation moved by 1% of the time
where the time goes in v3:
time: 32.7 us; the launch traced here: 32.6 us
  Pallas kernels  31.7 us (97%)
  local copies, waits for them, and re-layouts  0.82 us (3%)
    pallas_call x1, Pallas kernels, fused(): pl.pallas_call(kernel, out_shape=pltpu.VMEM((n, columns // n, channels),...  31.7 us
    unnamed x1, local copies, waits for them, and re-layouts  0.82 us

profile of v3, /device:TPU:9, one launch (start us, length us, event | category | flops | bytes accessed | tf_op | source)
XLA Modules:
  0.0 32.6 jit_solution(5072275666455060095)
XLA Ops:
  0.0 31.7 %shard_map.73 = bf16[16,48,384]{2,1,0:T(8,128)(2,1)S(1)} custom-call(bf16[16,48,384]{2,1,0:T(8,128)(2,1)} %bitcast.3, f32[384]{0:T(512)} %rg_hbm.1, bf16[384,1152]{1,0:T(8,128)(2,1)} %rqkv_hbm.1, bf16[384,384]{1,0:T(8,128)(2,1)} %rout_hbm.1, f32[384]{0:T(512)} %cg_hbm.1, bf16[384,1152]{1,0:T(8,128)(2,1)} %cqkv_hbm.1, bf16[384,384]{1,0:T(8,128)(2,1)} %cout_hbm.1), custom_call_target="tpu_custom_call" | custom-call | flops 3019898880 | bytes 2359296 | tf_op jit(solution)/shard_map/pallas_call | solution.py:309
  31.8 0.8 %copy.9 = bf16[1,768,384]{2,1,0:T(8,128)(2,1)} copy(bf16[1,768,384]{2,1,0:T(8,128)(2,1)S(1)} %bitcast.2) | data formatting | bytes 1179648

commit v4 on v3

--- a/solution.py
+++ b/solution.py
@@ -239,12 +239,15 @@
 
     def row_step(c, carry):
         row_across(c)
-        row_along(c - 1)
+        return carry
+
+    def row_rest(c, carry):
+        row_along(c)
         return carry
 
     row_across(0, 2)
     lax.fori_loop(1, chunks, row_step, 0)
-    row_along(chunks - 1)
+    lax.fori_loop(0, chunks, row_rest, 0)
     for copy in weights[3:]:
         copy.wait()
 

time: 32.7 us -> 32.8 us (level)
  no operation moved by 1% of the time
where the time goes in v4:
time: 32.8 us; the launch traced here: 32.7 us
  Pallas kernels  31.8 us (97%)
  local copies, waits for them, and re-layouts  0.82 us (2%)
    pallas_call x1, Pallas kernels, fused(): pl.pallas_call(kernel, out_shape=pltpu.VMEM((n, columns // n, channels),...  31.8 us
    unnamed x1, local copies, waits for them, and re-layouts  0.82 us

profile of v4, /device:TPU:9, one launch (start us, length us, event | category | flops | bytes accessed | tf_op | source)
XLA Modules:
  0.0 32.7 jit_solution(8407703422558464393)
XLA Ops:
  0.0 31.8 %shard_map.73 = bf16[16,48,384]{2,1,0:T(8,128)(2,1)S(1)} custom-call(bf16[16,48,384]{2,1,0:T(8,128)(2,1)} %bitcast.3, f32[384]{0:T(512)} %rg_hbm.1, bf16[384,1152]{1,0:T(8,128)(2,1)} %rqkv_hbm.1, bf16[384,384]{1,0:T(8,128)(2,1)} %rout_hbm.1, f32[384]{0:T(512)} %cg_hbm.1, bf16[384,1152]{1,0:T(8,128)(2,1)} %cqkv_hbm.1, bf16[384,384]{1,0:T(8,128)(2,1)} %cout_hbm.1), custom_call_target="tpu_custom_call" | custom-call | flops 3019898880 | bytes 2359296 | tf_op jit(solution)/shard_map/pallas_call | solution.py:312
  31.8 0.8 %copy.9 = bf16[1,768,384]{2,1,0:T(8,128)(2,1)} copy(bf16[1,768,384]{2,1,0:T(8,128)(2,1)S(1)} %bitcast.2) | data formatting | bytes 1179648
